TPU v7x, 768 devices: a whole 4x8x12 slice. The times are simulated.
768 devices in a mesh: row: 24 (over z, x_lo), col: 32 (over y, x_hi, core).
Axes of the slice: x: 4 (x_hi: 2, x_lo: 2; x = x_hi * 2 + x_lo), y: 8, z: 12, core: 2. Of those that a mesh axis runs over, the one named last changes fastest.
Arguments:
- densities: bfloat16 [30720, 4500], P('col'), may hold values from -0.75 to 0.75
- coupling_a: float32 [5, 900], replicated, may hold values from -6 to 6
- coupling_b: float32 [5, 900], replicated, may hold values from -6 to 6
- energies: float32 [30720], replicated, may hold values from 2 to 40
- strength: float32 [30720], replicated, may hold values from -6 to 6
- qp_index: int32 [30720, 2], replicated, may hold values from 0 to 1023
- kpi_label: int32 [30720], replicated, may hold values from 0 to 15
- amplitude_u: float32 [1024], replicated, may hold values from 0.1 to 1
- amplitude_v: float32 [1024], replicated, may hold values from 0.1 to 1
- panel_blocks: int32 [2], replicated, may hold values from 0 to 15, as said below
Outputs:
- matrix_a: float32 [2, 960, 30720], P(None, 'row', 'col')
- matrix_b: float32 [2, 960, 30720], P(None, 'row', 'col')
- response: float32 [2, 960], P(None, 'row')
- mirror: float32 [2, 30720], P(None, 'col')
Inputs may be any that keep to these rules, and one draw needn't show every extreme that they name: `panel_blocks`: both blocks lie in the lower half of the column blocks, one of them is block 15, and the two may coincide.
All inputs are finite; a program needn't handle non-finite values.
Results may differ from a plain program's by a relative error of at most 0.007.
Values may be sent and summed in bfloat16 or wider, within the bound.
A program may use at most 64 MiB of HBM per device.

v0:
```python
import math

import jax
import jax.numpy as jnp
from jax import lax
from jax.sharding import PartitionSpec as P

NKPI = 16


PAIRING = 1.0
HIGH = lax.Precision.HIGHEST


def from_root(x, axis, root):
    return lax.dynamic_index_in_dim(lax.all_gather(x, axis), root, 0, keepdims=False)


def sent_to_all(x, axis):
    size = lax.axis_size(axis)
    return lax.all_to_all(jnp.broadcast_to(x[None], (size, *x.shape)), axis, 0, 0, tiled=True)


def over_copies(x, axis):
    everything = sent_to_all(x, axis)
    return jnp.sum(everything, axis=0)


def pair_factors(qp_part, label_part, amplitude_u, amplitude_v):
    states = lax.broadcasted_iota(jnp.int32, (1, amplitude_u.shape[0]), 1)
    amp_table = jnp.stack([amplitude_u, amplitude_v], axis=1)
    first_amp = jnp.dot((qp_part[:, 0:1] == states).astype(jnp.float32), amp_table, precision=HIGH)
    second_amp = jnp.dot((qp_part[:, 1:2] == states).astype(jnp.float32), amp_table, precision=HIGH)
    anomal = first_amp[:, 0] * second_amp[:, 1] + first_amp[:, 1] * second_amp[:, 0]
    direct = first_amp[:, 0] * second_amp[:, 0] - first_amp[:, 1] * second_amp[:, 1]
    labels = lax.broadcasted_iota(jnp.int32, (1, NKPI), 1)
    member = (label_part[:, None] == labels).astype(jnp.float32)
    return (anomal, direct, member)


def on_device(
    densities,
    coupling_a,
    coupling_b,
    energies,
    strength,
    qp_index,
    kpi_label,
    amplitude_u,
    amplitude_v,
    panel_blocks,
):
    block_len = densities.shape[0]
    row_count = lax.axis_size("row")
    col_count = lax.axis_size("col")
    row_len = block_len // row_count
    row_pos = lax.axis_index("row")
    col_pos = lax.axis_index("col")
    total_pairs = block_len * col_count
    weight_a = coupling_a.reshape(-1)
    weight_b = coupling_b.reshape(-1)
    own_slice = lax.dynamic_slice_in_dim(densities, row_pos * row_len, row_len, 0)
    panel_one = from_root(own_slice, "col", panel_blocks[0])
    panel_two = from_root(own_slice, "col", panel_blocks[1])
    panels = (panel_one, panel_two)
    col_start = col_pos * block_len
    col_global = col_start + lax.broadcasted_iota(jnp.int32, (block_len,), 0)
    col_strength = lax.dynamic_slice_in_dim(strength, col_start, block_len, 0)
    col_anomal, col_direct, col_member = pair_factors(
        lax.dynamic_slice_in_dim(qp_index, col_start, block_len, 0),
        lax.dynamic_slice_in_dim(kpi_label, col_start, block_len, 0),
        amplitude_u,
        amplitude_v,
    )
    col_active = [col_pos >= panel_blocks[0], col_pos >= panel_blocks[1]]
    list_a, list_b, resp_parts, mirror_parts = ([], [], [], [])
    for which in range(2):
        block_id = panel_blocks[which]
        row_start = block_id * block_len + row_pos * row_len
        panel = panels[which]
        part_a = (panel * weight_a).astype(jnp.bfloat16)
        part_b = (panel * weight_b).astype(jnp.bfloat16)
        weighted = jnp.concatenate([part_a, part_b], 0)
        product = lax.dot_general(
            weighted, densities, (((1,), (1,)), ((), ())), preferred_element_type=jnp.float32
        )
        row_anomal, row_direct, row_member = pair_factors(
            lax.dynamic_slice_in_dim(qp_index, row_start, row_len, 0),
            lax.dynamic_slice_in_dim(kpi_label, row_start, row_len, 0),
            amplitude_u,
            amplitude_v,
        )
        row_energy = lax.dynamic_slice_in_dim(energies, row_start, row_len, 0)
        row_strength = lax.dynamic_slice_in_dim(strength, row_start, row_len, 0)
        pair_a = jnp.dot(
            row_anomal[:, None] * row_member, (col_anomal[:, None] * col_member).T, precision=HIGH
        )
        pair_b = jnp.dot(
            row_direct[:, None] * row_member, (col_direct[:, None] * col_member).T, precision=HIGH
        )
        row_global = row_start + lax.broadcasted_iota(jnp.int32, (row_len,), 0)
        diagonal = jnp.where(row_global[:, None] == col_global[None, :], row_energy[:, None], 0.0)
        mat_a = jnp.where(col_active[which], product[:row_len] + diagonal + PAIRING * pair_a, 0.0)
        mat_b = jnp.where(col_active[which], product[row_len:] + PAIRING * pair_b, 0.0)
        list_a.append(mat_a)
        list_b.append(mat_b)
        summed = mat_a + mat_b
        resp_parts.append(jnp.dot(summed, col_strength, precision=HIGH))
        mirror_parts.append(jnp.dot(row_strength, summed, precision=HIGH))
    response = over_copies(jnp.stack(resp_parts), "col") / math.sqrt(total_pairs)
    mirror = over_copies(jnp.stack(mirror_parts), "row") / math.sqrt(block_len)
    return (jnp.stack(list_a), jnp.stack(list_b), response, mirror)


def solution(mesh):
    placed = (P("col", None), P(), P(), P(), P(), P(), P(), P(), P(), P())
    return jax.shard_map(
        on_device,
        mesh=mesh,
        in_specs=placed,
        out_specs=(P(None, "row", "col"), P(None, "row", "col"), P(None, "row"), P(None, "col")),
        check_vma=False,
    )
```

profile of v0, /device:TPU:6, one launch (start us, length us, event | category | flops | bytes accessed | tf_op | source)
XLA Modules:
  0.0 205.4 jit_solution(6274027982327853672)
XLA Ops:
  7.2 1.7 constant_dynamic-slice_fusion.3
  9.0 1.3 fusion.80
  15.5 0.8 mul.163
  16.4 0.8 mul.166
  17.2 0.8 dynamic_slice.48
  19.4 0.8 fusion.78
  20.2 0.8 fusion.79
  21.0 0.8 constant_dynamic-slice_fusion.2
  21.7 0.9 constant_dynamic-slice_fusion
  22.6 0.9 fusion.36
  23.5 1.0 fusion.37
  24.5 1.0 fusion.38
  25.4 1.0 fusion.39
  26.5 2.6 %fusion = f32[960,2]{0,1:T(2,128)S(1)} fusion(s32[960]{0:T(1024)S(1)} %bitcast.61, f32[1024,1]{0,1:T(1,128)} %bitcast.70, f32[1024,1]{0,1:T(1,128)} %bitcast.76), kind=kOutput, calls=%fused_computation.2 | convolution fusion | flops 24578048 | bytes 19712 | tf_op jit(solution)/shard_map/dot_general | solution.py:32
  29.0 2.6 %fusion.1 = f32[960,2]{0,1:T(2,128)S(1)} fusion(s32[960]{0:T(1024)S(1)} %bitcast.60, f32[1024,1]{0,1:T(1,128)} %bitcast.71, f32[1024,1]{0,1:T(1,128)} %bitcast.77), kind=kOutput, calls=%fused_computation.3 | convolution fusion | flops 24578048 | bytes 19712 | tf_op jit(solution)/shard_map/dot_general | solution.py:33
  31.7 109.8 %all-gather.3.cloned.1.call-done = bf16[1280,4500]{1,0:T(8,128)(2,1)} async-done(((bf16[40,4500]{1,0:T(8,128)(2,1)}), bf16[1280,4500]{1,0:T(8,128)(2,1)}) %all-gather.3.cloned.1.call-update) | async-done | bytes 11520016 | tf_op jit(solution)/shard_map/all_gather | solution.py:16
  141.5 1.4 fusion.8
  142.9 6.5 %fusion.12 = f32[80,960]{1,0:T(8,128)S(1)} fusion(bf16[960,4500]{1,0:T(8,128)(2,1)} %param.10, bf16[40,4500]{1,0:T(8,128)(2,1)S(1)} %get-tuple-element.9, bf16[40,4500]{1,0:T(8,128)(2,1)S(1)} %get-tuple-element.4), kind=kOutput, calls=%fused_computation.22 | convolution fusion | flops 692640000 | bytes 9667200 | tf_op jit(solution)/shard_map/dot_general | solution.py:84
  149.4 0.9 fusion.5
  150.3 0.9 fusion.7
  151.6 2.8 %fusion.16 = f32[80,960]{1,0:T(8,128)S(1)} fusion(bf16[960,4500]{1,0:T(8,128)(2,1)S(1)} %copy-done.1, bf16[40,4500]{1,0:T(8,128)(2,1)S(1)} %get-tuple-element.8, bf16[40,4500]{1,0:T(8,128)(2,1)S(1)} %get-tuple-element.5), kind=kOutput, calls=%fused_computation.26 | convolution fusion | flops 692640000 | bytes 9667200 | tf_op jit(solution)/shard_map/dot_general | solution.py:84
  154.4 0.9 fusion.4
  155.3 0.9 fusion.6
  156.7 0.6 broadcast_in_dim.30
  157.3 7.4 %all-to-all-start = ((f32[32,2,40]{2,1,0:T(2,128)}), f32[32,2,40]{2,1,0:T(2,128)S(1)}, u32[]{:S(2)}, u32[]{:S(2)}) async-start(f32[32,2,40]{2,1,0:T(2,128)} %broadcast_in_dim.30), calls=%async_computation | async-start | bytes 65536 | tf_op jit(solution)/shard_map/all_to_all | solution.py:21
  164.8 7.3 %all-to-all-done = f32[32,2,40]{2,1,0:T(2,128)S(1)} async-done(((f32[32,2,40]{2,1,0:T(2,128)}), f32[32,2,40]{2,1,0:T(2,128)S(1)}, u32[]{:S(2)}, u32[]{:S(2)}) %all-to-all-start) | async-done | bytes 10272 | tf_op jit(solution)/shard_map/all_to_all | solution.py:21
  172.1 0.7 broadcast_in_dim.31
  172.8 11.7 %all-to-all-start.1 = ((f32[24,2,960]{2,1,0:T(2,128)}), f32[24,2,960]{2,1,0:T(2,128)S(1)}, u32[]{:S(2)}, u32[]{:S(2)}) async-start(f32[24,2,960]{2,1,0:T(2,128)} %broadcast_in_dim.31), calls=%async_computation.1 | async-start | bytes 393216 | tf_op jit(solution)/shard_map/all_to_all | solution.py:21
  184.5 0.7 pad_maximum_fusion.1
  185.3 0.7 pad_maximum_fusion
  186.6 11.2 %all-to-all-done.1 = f32[24,2,960]{2,1,0:T(2,128)S(1)} async-done(((f32[24,2,960]{2,1,0:T(2,128)}), f32[24,2,960]{2,1,0:T(2,128)S(1)}, u32[]{:S(2)}, u32[]{:S(2)}) %all-to-all-start.1) | async-done | bytes 184352 | tf_op jit(solution)/shard_map/all_to_all | solution.py:21
  197.9 0.6 broadcast_multiply_fusion
  (23 shorter events, 2.0 us)
Async XLA Ops:
  7.2 10.8 %copy-start = (f32[30720]{0:T(1024)S(1)}, f32[30720]{0:T(1024)}, u32[]{:S(2)}) copy-start(f32[30720]{0:T(1024)} %param.14) | copy-start | bytes 368644
  7.2 134.3 %all-gather.3.cloned.1.call-start = ((), (), s32[]{:S(2)}) async-start(), calls=%async_computation.2 | async-start | bytes 12165120 | tf_op jit(solution)/shard_map/all_gather | solution.py:16
  141.5 10.2 %copy-start.1 = (bf16[960,4500]{1,0:T(8,128)(2,1)S(1)}, bf16[960,4500]{1,0:T(8,128)(2,1)}, u32[]{:S(2)}) copy-start(bf16[960,4500]{1,0:T(8,128)(2,1)} %param.10) | copy-start | bytes 25920004
  157.3 14.8 %all-to-all-start = ((f32[32,2,40]{2,1,0:T(2,128)}), f32[32,2,40]{2,1,0:T(2,128)S(1)}, u32[]{:S(2)}, u32[]{:S(2)}) async-start(f32[32,2,40]{2,1,0:T(2,128)} %broadcast_in_dim.30), calls=%async_computation | async-start | bytes 65536 | tf_op jit(solution)/shard_map/all_to_all | solution.py:21
  172.8 25.0 %all-to-all-start.1 = ((f32[24,2,960]{2,1,0:T(2,128)}), f32[24,2,960]{2,1,0:T(2,128)S(1)}, u32[]{:S(2)}, u32[]{:S(2)}) async-start(f32[24,2,960]{2,1,0:T(2,128)} %broadcast_in_dim.31), calls=%async_computation.1 | async-start | bytes 393216 | tf_op jit(solution)/shard_map/all_to_all | solution.py:21
Sparse Core Ops, SparseCore 0:
  11.9 129.5 all-gather.2
where the time goes:
time: 208 us; the launch traced here: 205 us
  waiting for transfers between devices  128 us (62%)
  matrix products  22.6 us (11%)
  between operations  20.7 us (10%)
  starting transfers between devices  19.2 us (9%)
  local copies, waits for them, and re-layouts  10.2 us (5%)
  other arithmetic  4.43 us (2%)
    all_gather x1, waiting for transfers between devices, from_root(): lax.all_gather(x, axis)  110 us
    all_to_all x2, starting transfers between devices, sent_to_all(): lax.all_to_all(jnp.broadcast_to(x[None], (size, *x.shape)), axis, 0, 0, t...  19.1 us
    all_to_all x2, waiting for transfers between devices, sent_to_all(): lax.all_to_all(jnp.broadcast_to(x[None], (size, *x.shape)), axis, 0, 0, t...  18.6 us
    dot_general x2, matrix products, on_device(): lax.dot_general(weighted, densities, (((1,), (1,)), ((), ())), preferred_...  9.27 us
    dot_general x3, matrix products, pair_factors(): jnp.dot((qp_part[:, 1:2] == states).astype(jnp.float32), amp_table, preci...  4.52 us
    dot_general x3, matrix products, pair_factors(): jnp.dot((qp_part[:, 0:1] == states).astype(jnp.float32), amp_table, preci...  4.42 us
  transfers between devices with their start and end apart: 3, of which 3 were waited for; matrix products, arithmetic and copies ran while one was open for 9% of the time, Pallas kernels for 0%

commit v1 on v0

v1 whole, which is shorter than its diff:
```python
import functools
import math

import jax
import jax.numpy as jnp
from jax import lax
from jax.experimental import pallas as pl
from jax.experimental.pallas import tpu as pltpu
from jax.sharding import PartitionSpec as P

PAIRING = 1.0
TOP = 15
UPPER = 4
CHUNKS = 5
MESH_ID = pl.DeviceIdType.MESH


def both(*conds):
    out = conds[0]
    for cond in conds[1:]:
        out = jnp.logical_and(out, cond)
    return out


def spread_kernel(block, dens, out, buf, recv_sem, send_sem, local_sem):
    row = lax.axis_index("row")
    col = lax.axis_index("col")
    other = row + 1 - 2 * lax.rem(row, 2)
    level = col // 4
    half = lax.rem(col // 2, 2)
    core = lax.rem(col, 2)
    row_len = buf.shape[1]
    size = row_len // CHUNKS

    src_level, src_half, src_core = block // 4, (block // 2) % 2, block % 2
    here = (src_level, src_half, src_core)

    top_src = col == TOP
    top_recv = level >= UPPER
    from_src = jnp.logical_and(level == UPPER, core == 1)
    top_from_row = jnp.where(jnp.logical_and(from_src, half == 0), other, row)
    top_from_col = jnp.where(core == 0, col + 1, jnp.where(from_src, TOP, col - 4))
    top_up = both(core == 1, level >= UPPER, level < 7)
    top_mate = both(core == 1, level >= UPPER)

    same = block == TOP
    src = col == block
    root_col = src_level * 4 + (1 - src_half) * 2
    root = col == root_col
    up_dst = both(level > src_level, level < UPPER)
    relay_zero = jnp.logical_and(src_level == 3, both(level == 0, core == 0))
    root_needs = jnp.logical_and(col > block, level == src_level)
    recv = jnp.logical_or(jnp.logical_or(col > block, root), relay_zero)
    if same:
        recv = col < 0
        src = col < 0
        root = col < 0
    src_dev = jnp.where(half == src_half, block, root_col)
    on_mate = jnp.logical_and(core == 1, col > block)
    if src_level == 3:
        entry_up = col < 0
        entry_down = both(level == 0, core == 0)
        from_zero = both(level == 7, core == 0)
    else:
        entry_up = both(level == src_level + 1, core == 0)
        entry_down = both(level == 7, core == 0)
        from_zero = col < 0
    from_col = jnp.where(
        root,
        block,
        jnp.where(
            on_mate,
            col - 1,
            jnp.where(
                jnp.logical_or(entry_up, entry_down),
                src_dev,
                jnp.where(from_zero, half * 2, jnp.where(level >= UPPER, col + 4, col - 4)),
            ),
        ),
    )
    from_row = jnp.where(root, other, row)
    start = jnp.logical_or(src, root)
    down_entry_col = (0 if src_level == 3 else 28) + half * 2
    none = col < 0
    if same:
        sends = []
        root_send = none
    else:
        up_relay = both(core == 0, level > src_level, level < 3)
        start_up = start if src_level < 3 else none
        up = jnp.logical_or(start_up, up_relay)
        up_col = jnp.where(start, (src_level + 1) * 4 + half * 2, col + 4)
        down_relay = both(core == 0, level > UPPER)
        zero_relay = both(core == 0, level == 0) if src_level == 3 else none
        down = jnp.logical_or(jnp.logical_or(start, down_relay), zero_relay)
        down_col = jnp.where(start, down_entry_col, jnp.where(zero_relay, 28 + half * 2, col - 4))
        mate = jnp.logical_and(core == 0, col >= block)
        sends = [(up, up_col), (down, down_col), (mate, col + 1)]
        root_send = src

    barrier = pltpu.get_barrier_semaphore()

    @pl.when(top_recv)
    def _():
        pl.semaphore_signal(barrier, 1, device_id=(top_from_row, top_from_col), device_id_type=MESH_ID)

    @pl.when(recv)
    def _():
        pl.semaphore_signal(barrier, 1, device_id=(from_row, from_col), device_id_type=MESH_ID)

    one = lambda cond: jnp.where(cond, 1, 0)
    count = 2 * one(top_src) + one(top_up) + one(top_mate) + one(root_send)
    for cond, _ in sends:
        count = count + one(cond)

    @pl.when(count > 0)
    def _():
        pl.semaphore_wait(barrier, count)

    def part(j):
        return pl.ds(j * size, size)

    def copy(which, slot, j, src_ref, to_row, to_col):
        return pltpu.make_async_remote_copy(
            src_ref=src_ref,
            dst_ref=buf.at[which, part(j)],
            send_sem=send_sem.at[which, slot, j],
            recv_sem=recv_sem.at[which, j],
            device_id=(to_row, to_col),
            device_id_type=MESH_ID,
        )

    def own(r, j):
        return dens.at[pl.ds(pl.multiple_of(r * row_len + j * size, 8), size)]

    def held(which, j):
        return buf.at[which, part(j)]

    def keep(which):
        return pltpu.make_async_copy(
            dens.at[pl.ds(pl.multiple_of(row * row_len, 8), row_len)], buf.at[which], local_sem.at[which]
        )

    for j in range(CHUNKS):

        @pl.when(top_src)
        def _():
            copy(0, 0, j, own(row, j), row, UPPER * 4 + 3).start()
            copy(0, 1, j, own(other, j), other, UPPER * 4 + 1).start()

        @pl.when(src)
        def _():
            for slot, (cond, to_col) in enumerate(sends):

                @pl.when(cond)
                def _():
                    copy(1, slot, j, own(row, j), row, to_col).start()

            copy(1, 3, j, own(other, j), other, root_col).start()

    @pl.when(top_src)
    def _():
        keep(0).start()

    @pl.when(src)
    def _():
        keep(1).start()

    relay_one = jnp.logical_and(recv, core == 0)
    for j in range(CHUNKS):
        if not same:

            @pl.when(relay_one)
            def _():
                copy(1, 0, j, held(1, j), row, col).wait_recv()
                for slot, (cond, to_col) in enumerate(sends):

                    @pl.when(cond)
                    def _():
                        copy(1, slot, j, held(1, j), row, to_col).start()

        @pl.when(top_mate)
        def _():
            copy(0, 0, j, held(0, j), row, col).wait_recv()
            copy(0, 0, j, held(0, j), row, col - 1).start()

            @pl.when(top_up)
            def _():
                copy(0, 1, j, held(0, j), row, col + 4).start()

    for j in range(CHUNKS):

        @pl.when(both(top_recv, core == 0))
        def _():
            copy(0, 0, j, held(0, j), row, col).wait_recv()

        if not same:

            @pl.when(jnp.logical_and(recv, core == 1))
            def _():
                copy(1, 0, j, held(1, j), row, col).wait_recv()

    @pl.when(top_src)
    def _():
        keep(0).wait()

    @pl.when(src)
    def _():
        keep(1).wait()

    write = pltpu.make_async_copy(buf, out, local_sem.at[2])
    write.start()

    for j in range(CHUNKS):

        @pl.when(top_src)
        def _():
            copy(0, 0, j, held(0, j), row, col).wait_send()
            copy(0, 1, j, held(0, j), row, col).wait_send()

        @pl.when(top_mate)
        def _():
            copy(0, 0, j, held(0, j), row, col).wait_send()

        @pl.when(top_up)
        def _():
            copy(0, 1, j, held(0, j), row, col).wait_send()

        if not same:
            for slot, (cond, _) in enumerate(sends):

                @pl.when(cond)
                def _():
                    copy(1, slot, j, held(1, j), row, col).wait_send()

            @pl.when(src)
            def _():
                copy(1, 3, j, held(1, j), row, col).wait_send()

    write.wait()


def spread(block, row_len, dens):
    features = dens.shape[1]
    return pl.pallas_call(
        functools.partial(spread_kernel, block),
        name=f"spread_{block}",
        out_shape=jax.ShapeDtypeStruct((2, row_len, features), dens.dtype),
        in_specs=[pl.BlockSpec(memory_space=pl.ANY)],
        out_specs=pl.BlockSpec(memory_space=pl.ANY),
        scratch_shapes=[
            pltpu.VMEM((2, row_len, features), dens.dtype),
            pltpu.SemaphoreType.DMA((2, CHUNKS)),
            pltpu.SemaphoreType.DMA((2, 4, CHUNKS)),
            pltpu.SemaphoreType.DMA((3,)),
        ],
        compiler_params=pltpu.CompilerParams(collective_id=block, has_side_effects=True),
    )(dens)


def split3(x):
    hi = x.astype(jnp.bfloat16)
    rest = x - hi.astype(jnp.float32)
    mid = rest.astype(jnp.bfloat16)
    low = (rest - mid.astype(jnp.float32)).astype(jnp.bfloat16)
    return hi, mid, low


def dot_t(a, b):
    return lax.dot_general(a, b, (((1,), (1,)), ((), ())), preferred_element_type=jnp.float32)


def pick(table, index):
    states = table.shape[1]
    hit = lax.broadcasted_iota(jnp.int32, (states, index.shape[1]), 0) == index
    hit = jnp.where(hit, 1.0, 0.0).astype(jnp.bfloat16)
    parts = jnp.dot(table, hit, preferred_element_type=jnp.float32)
    u = parts[0:1] + parts[1:2] + parts[2:3]
    v = parts[3:4] + parts[4:5] + parts[5:6]
    return u, v


def compute_kernel(
    blocks,
    panels,
    dens,
    coup_a,
    coup_b,
    energies,
    strength,
    qp,
    label,
    amp_u,
    amp_v,
    mat_a,
    mat_b,
    resp_part,
    mir_part,
    weight,
    acc,
):
    row = lax.axis_index("row")
    col = lax.axis_index("col")
    row_len = panels.shape[1]
    block_len = dens.shape[0]
    features = dens.shape[1]

    types, points = coup_a.shape
    for t in range(types):
        weight[0:1, t * points : (t + 1) * points] = coup_a[t : t + 1, :]
        weight[1:2, t * points : (t + 1) * points] = coup_b[t : t + 1, :]

    slot = [jnp.where(blocks[k] == TOP, 0, 1) for k in range(2)]

    step = 512
    acc[...] = jnp.zeros_like(acc)

    def product(lo, size):
        at = pl.ds(lo, size)
        wa = weight[0:1, at]
        wb = weight[1:2, at]
        stack = []
        for k in range(2):
            p = panels[slot[k], :, at].astype(jnp.float32)
            stack += [p * wa, p * wb]
        weighted = jnp.concatenate(stack, 0).astype(jnp.bfloat16)
        acc[...] += dot_t(weighted, dens[:, at])

    def body(i, _):
        product(pl.multiple_of(i * step, step), step)
        return 0

    full = features // step
    lax.fori_loop(0, full, body, 0)
    product(full * step, features - full * step)

    odd = lax.rem(col, 2) == 1
    base = pl.multiple_of(col * block_len - jnp.where(odd, 64, 0), 128)
    wide = pl.ds(base, block_len + 64)

    def own(ref):
        x = ref[:, wide]
        return jnp.where(odd, x[:, 64:], x[:, :block_len])

    table = jnp.concatenate(
        [t.astype(jnp.float32) for t in (*split3(amp_u[...]), *split3(amp_v[...]))] + [jnp.zeros((2, amp_u.shape[1]), jnp.float32)], 0
    ).astype(jnp.bfloat16)

    def factors(pairs):
        u_i, v_i = pick(table, pairs[0:1])
        u_j, v_j = pick(table, pairs[1:2])
        return u_i * v_j + v_i * u_j, u_i * u_j - v_i * v_j

    col_anomal, col_direct = factors(own(qp))
    col_label = own(label)
    col_strength = own(strength)
    col_global = col * block_len + lax.broadcasted_iota(jnp.int32, (1, block_len), 1)

    sums = []
    for k in range(2):
        first = blocks[k] * block_len + row * row_len
        near = pl.multiple_of(first // 128 * 128, 128)
        shift = first - near

        def rows_of(ref):
            x = pltpu.roll(ref[:, pl.ds(near, 256)], 256 - shift, axis=1)
            return x[:, :128]

        row_anomal, row_direct = factors(rows_of(qp))
        packed = jnp.concatenate(
            [
                row_anomal,
                row_direct,
                rows_of(label).astype(jnp.float32),
                rows_of(energies),
                rows_of(strength),
                jnp.zeros((3, 128), jnp.float32),
            ],
            0,
        )
        tall = packed.T[:row_len]
        anomal, direct, lab, energy, stren = (tall[:, i : i + 1] for i in range(5))
        row_global = first + lax.broadcasted_iota(jnp.int32, (row_len, 1), 0)
        active = col >= blocks[k]
        agree = lab == col_label.astype(jnp.float32)
        prod_a = acc[2 * k * row_len : (2 * k + 1) * row_len]
        prod_b = acc[(2 * k + 1) * row_len : (2 * k + 2) * row_len]
        a = prod_a + jnp.where(row_global == col_global, energy, 0.0)
        a = a + PAIRING * jnp.where(agree, anomal * col_anomal, 0.0)
        b = prod_b + PAIRING * jnp.where(agree, direct * col_direct, 0.0)
        a = jnp.where(active, a, 0.0)
        b = jnp.where(active, b, 0.0)
        mat_a[k] = a
        mat_b[k] = b
        both_ab = a + b
        sums.append(both_ab)
        mir_part[k : k + 1, :] = jnp.sum(both_ab * stren, axis=0, keepdims=True)
    summed = jnp.concatenate(sums, 0)
    resp = jnp.sum(summed * col_strength, axis=1, keepdims=True)
    wide_resp = jnp.concatenate([resp, jnp.zeros((128 - 2 * row_len, 1), jnp.float32)], 0)
    wide_resp = jnp.broadcast_to(wide_resp, (128, 8 * 16)).T
    resp_part[...] = wide_resp[0:1]


def reduce_kernel(
    resp_in,
    mir_in,
    response,
    mirror,
    resp_all,
    mir_pair,
    mir_all,
    resp_send,
    resp_recv,
    pair_send,
    pair_recv,
    mir_send,
    mir_recv,
):
    row = lax.axis_index("row")
    col = lax.axis_index("col")
    rows = lax.axis_size("row")
    cols = lax.axis_size("col")
    other = row + 1 - 2 * lax.rem(row, 2)
    deep = rows // 2
    z = row // 2
    row_len = response.shape[1]
    block_len = mirror.shape[1]
    total = block_len * cols

    barrier = pltpu.get_barrier_semaphore()

    def greet_col(d, _):
        pl.semaphore_signal(barrier, 1, device_id=(row, lax.rem(col + d, cols)), device_id_type=MESH_ID)
        return 0

    def greet_deep(d, _):
        to = lax.rem(z + d, deep) * 2 + lax.rem(row, 2)
        pl.semaphore_signal(barrier, 1, device_id=(to, col), device_id_type=MESH_ID)
        return 0

    lax.fori_loop(1, cols, greet_col, 0)
    lax.fori_loop(1, deep, greet_deep, 0)
    pl.semaphore_signal(barrier, 1, device_id=(other, col), device_id_type=MESH_ID)

    resp_all[col] = resp_in[...]
    mir_pair[0] = mir_in[...]
    pl.semaphore_wait(barrier, cols - 1 + deep - 1 + 1)

    def send_resp(d, _):
        pltpu.make_async_remote_copy(
            src_ref=resp_all.at[col],
            dst_ref=resp_all.at[col],
            send_sem=resp_send,
            recv_sem=resp_recv,
            device_id=(row, lax.rem(col + d, cols)),
            device_id_type=MESH_ID,
        ).start()
        return 0

    pair = pltpu.make_async_remote_copy(
        src_ref=mir_pair.at[0],
        dst_ref=mir_pair.at[1],
        send_sem=pair_send,
        recv_sem=pair_recv,
        device_id=(other, col),
        device_id_type=MESH_ID,
    )
    pair.start()
    lax.fori_loop(1, cols, send_resp, 0)
    pair.wait_recv()
    mir_all[z] = mir_pair[0] + mir_pair[1]

    def send_mir(d, _):
        to = lax.rem(z + d, deep) * 2 + lax.rem(row, 2)
        pltpu.make_async_remote_copy(
            src_ref=mir_all.at[z],
            dst_ref=mir_all.at[z],
            send_sem=mir_send,
            recv_sem=mir_recv,
            device_id=(to, col),
            device_id_type=MESH_ID,
        ).start()
        return 0

    lax.fori_loop(1, deep, send_mir, 0)

    def wait_all(ref, count, sem):
        some = ref.at[pl.ds(0, count)]
        pltpu.make_async_copy(some, some, sem).wait()

    wait_all(resp_all, cols - 1, resp_recv)
    r = jnp.sum(resp_all[...], axis=0) * (1.0 / math.sqrt(total))
    response[0:1, :] = r[:, :row_len]
    response[1:2, :] = r[:, row_len : 2 * row_len]
    wait_all(mir_all, deep - 1, mir_recv)
    m = jnp.sum(mir_all[...], axis=0) * (1.0 / math.sqrt(block_len))
    mirror[...] = m
    wait_all(resp_all, cols - 1, resp_send)
    wait_all(mir_all, deep - 1, mir_send)
    pair.wait_send()


def compute(panels, dens, coup_a, coup_b, energies, strength, qp, label, amp_u, amp_v, blocks):
    row_len, features = panels.shape[1:]
    block_len = dens.shape[0]
    vmem = pl.BlockSpec(memory_space=pltpu.VMEM)
    out = jax.ShapeDtypeStruct
    f32 = jnp.float32
    return pl.pallas_call(
        compute_kernel,
        name="compute",
        out_shape=(
            out((2, row_len, block_len), f32),
            out((2, row_len, block_len), f32),
            out((1, 128), f32),
            out((2, block_len), f32),
        ),
        in_specs=[pl.BlockSpec(memory_space=pltpu.SMEM)] + [vmem] * 10,
        out_specs=(vmem,) * 4,
        scratch_shapes=[
            pltpu.VMEM((8, features), f32),
            pltpu.VMEM((4 * row_len, block_len), f32),
        ],
        compiler_params=pltpu.CompilerParams(vmem_limit_bytes=24 * 1024 * 1024),
    )(blocks, panels, dens, coup_a, coup_b, energies, strength, qp, label, amp_u, amp_v)


def reduce(rows, cols, row_len, resp_part, mir_part):
    block_len = mir_part.shape[1]
    vmem = pl.BlockSpec(memory_space=pltpu.VMEM)
    out = jax.ShapeDtypeStruct
    f32 = jnp.float32
    return pl.pallas_call(
        reduce_kernel,
        name="reduce",
        out_shape=(out((2, row_len), f32), out((2, block_len), f32)),
        in_specs=[vmem, vmem],
        out_specs=(vmem, vmem),
        scratch_shapes=[
            pltpu.VMEM((cols, 1, 128), f32),
            pltpu.VMEM((2, 2, block_len), f32),
            pltpu.VMEM((rows // 2, 2, block_len), f32),
        ]
        + [pltpu.SemaphoreType.DMA] * 6,
        compiler_params=pltpu.CompilerParams(collective_id=TOP + 1, has_side_effects=True),
    )(resp_part, mir_part)


def on_device(
    densities, coupling_a, coupling_b, energies, strength, qp_index, kpi_label, amplitude_u, amplitude_v, panel_blocks
):
    rows = lax.axis_size("row")
    cols = lax.axis_size("col")
    row_len = densities.shape[0] // rows
    moving = panel_blocks[0] + panel_blocks[1] - TOP
    branches = [functools.partial(spread, block, row_len) for block in range(TOP + 1)]
    panels = lax.switch(moving, branches, densities)
    flat = lambda x: x.reshape(1, -1)
    a, b, resp_part, mir_part = compute(
        panels,
        densities,
        coupling_a,
        coupling_b,
        flat(energies),
        flat(strength),
        qp_index.T,
        flat(kpi_label),
        flat(amplitude_u),
        flat(amplitude_v),
        panel_blocks,
    )
    response, mirror = reduce(rows, cols, row_len, resp_part, mir_part)
    return a, b, response, mirror


def solution(mesh):
    placed = (P("col", None), P(), P(), P(), P(), P(), P(), P(), P(), P())
    return jax.shard_map(
        on_device,
        mesh=mesh,
        in_specs=placed,
        out_specs=(P(None, "row", "col"), P(None, "row", "col"), P(None, "row"), P(None, "col")),
        check_vma=False,
    )
```

time: 208 us -> 72.3 us (0.35); the launches traced: 205 us -> 73.2 us
  waiting for transfers between devices: 128 us -> 0 us
  Pallas kernels: 0 us -> 65.9 us
  matrix products: 22.6 us -> 0 us
  starting transfers between devices: 19.2 us -> 0 us
  between operations: 20.7 us -> 2.09 us
  local copies, waits for them, and re-layouts: 10.2 us -> 5 us
  other arithmetic: 4.43 us -> 0 us
    all_gather x1 -> x0, waiting for transfers between devices: 110 us -> none  [from_root(): lax.all_gather(x, axis)]
    pallas_call x0 -> x3, Pallas kernels: none -> 65.9 us  [the longest x1 41.9 us: reduce(): pl.pallas_call(reduce_kernel, name='reduce', out_shape=(out((2, row_len),...]
    dot_general x16 -> x0, matrix products: 22.6 us -> none  [the longest x2 9.27 us: on_device(): lax.dot_general(weighted, densities, (((1,), (1,)), ((), ())), preferred_...]
    all_to_all x2 -> x0, starting transfers between devices: 19.1 us -> none  [sent_to_all(): lax.all_to_all(jnp.broadcast_to(x[None], (size, *x.shape)), axis, 0, 0, t...]
    all_to_all x2 -> x0, waiting for transfers between devices: 18.6 us -> none  [sent_to_all(): lax.all_to_all(jnp.broadcast_to(x[None], (size, *x.shape)), axis, 0, 0, t...]
    dynamic_slice x6 -> x0, local copies, waits for them, and re-layouts: 4.96 us -> none  [the longest x1 1.75 us: on_device(): lax.dynamic_slice_in_dim(densities, row_pos * row_len, row_len, 0)]
    unnamed x4 -> x24, local copies, waits for them, and re-layouts: 0.01 us -> 3.69 us
  transfers between devices with their start and end apart: 3 -> 0, of which waited for: 3 -> 0; matrix products, arithmetic and copies ran while one was open for 9% -> 0% of each run, Pallas kernels for 0% -> 0%
where the time goes in v1:
time: 72.3 us; the launch traced here: 73.2 us
  Pallas kernels  65.9 us (91%)
  local copies, waits for them, and re-layouts  5 us (7%)
  between operations  2.09 us (3%)
    pallas_call x1, Pallas kernels, reduce(): pl.pallas_call(reduce_kernel, name='reduce', out_shape=(out((2, row_len),...  41.9 us
    pallas_call x1, Pallas kernels, spread(): pl.pallas_call(functools.partial(spread_kernel, block), name=f'spread_{bl...  13.1 us
    pallas_call x1, Pallas kernels, compute(): pl.pallas_call(compute_kernel, name='compute', out_shape=(out((2, row_len...  10.8 us
    unnamed x24, local copies, waits for them, and re-layouts  3.69 us

profile of v1, /device:TPU:6, one launch (start us, length us, event | category | flops | bytes accessed | tf_op | source)
XLA Modules:
  0.0 73.2 jit_solution(15585553421532322704)
XLA Ops:
  0.6 1.3 %fusion = (s32[1]{0:T(128)}, s32[1]{0:T(128)}) fusion(s32[2]{0:T(128)} %blocks.1), kind=kLoop, calls=%fused_computation | loop fusion | bytes 16 | tf_op jit(solution)/shard_map/slice | solution.py:556
  3.2 0.0 copy-start
  3.3 0.0 copy-start.1
  3.3 0.0 copy-start.2
  3.3 0.0 copy-start.3
  3.3 0.0 copy-start.4
  3.3 0.0 copy-start.5
  3.3 0.0 copy-start.7
  3.3 0.0 copy-start.8
  3.3 0.0 copy-start.9
  3.4 13.4 %conditional.1 = (bf16[2,40,4500]{2,1,0:T(8,128)(2,1)S(1)}) conditional(s32[]{:T(128)} %bitcast, bf16[960,4500]{1,0:T(8,128)(2,1)} %dens.17, bf16[960,4500]{1,0:T(8,128)(2,1)} %dens.17, bf16[960,4500]{1,0:T(8,128)(2,1)} %dens.17, bf16[960,4500]{1,0:T(8,128)(2,1)} %dens.17, bf16[960,4500]{1,0:T(8,128)(2,1)} %dens.17, ...), branch_computations={%region_0.0_spmd, %region_1.0_spmd, %region_2.0_spmd, %region_3.0_... | conditional | bytes 8 | solution.py:558
  3.4 13.1 %spread_14.1 = bf16[2,40,4500]{2,1,0:T(8,128)(2,1)S(1)} custom-call(bf16[960,4500]{1,0:T(8,128)(2,1)} %dens.15), custom_call_target="tpu_custom_call" | custom-call | tf_op jit(solution)/shard_map/cond/branch_14_fun/spread_14/pallas_call | solution.py:245
  16.7 0.0 copy-done
  16.7 0.0 copy-done.1
  16.8 0.0 copy-done.2
  16.8 0.0 copy-done.3
  16.8 0.0 copy-done.4
  16.8 0.0 copy-done.5
  16.8 0.0 copy-done.7
  16.8 0.0 copy-done.8
  16.8 0.0 copy-done.9
  16.8 10.8 %compute.1 = (f32[2,40,960]{2,1,0:T(8,128)}, f32[2,40,960]{2,1,0:T(8,128)}, f32[1,128]{1,0:T(1,128)S(1)}, f32[2,960]{1,0:T(2,128)S(1)}) custom-call(s32[2]{0:T(128)S(1)} %copy-done.7, bf16[2,40,4500]{2,1,0:T(8,128)(2,1)S(1)} %get-tuple-element.59.panels, bf16[960,4500]{1,0:T(8,128)(2,1)} %dens.17, f32[5,900]{1,0:T(8,128)S(1)} %copy-done.4, ...), custom_call_target="tpu_custom_call" | custom-call | tf_op jit(solution)/shard_map/compute/pallas_call | solution.py:510
  27.7 0.0 copy-start.6
  27.7 0.6 copy-done.6
  28.3 0.0 copy-start.10
  28.3 0.5 copy-done.10
  28.8 41.9 %reduce.1 = (f32[2,40]{1,0:T(2,128)}, f32[2,960]{1,0:T(2,128)}) custom-call(f32[1,128]{1,0:T(1,128)} %copy-done.10, f32[2,960]{1,0:T(2,128)} %copy-done.6), custom_call_target="tpu_custom_call" | custom-call | tf_op jit(solution)/shard_map/reduce/pallas_call | solution.py:534
  70.7 1.2 %copy.32 = f32[2,40]{1,0:T(2,128)} copy(f32[2,40]{1,0:T(2,128)} %get-tuple-element.57) | data formatting | bytes 640
  71.9 1.3 %copy.33 = f32[2,960]{1,0:T(2,128)} copy(f32[2,960]{1,0:T(2,128)} %get-tuple-element.58) | data formatting | bytes 15360
Async XLA Ops:
  3.2 13.5 %copy-start = (s32[30720,2]{0,1:T(2,128)S(1)}, s32[30720,2]{0,1:T(2,128)}, u32[]{:S(2)}) copy-start(s32[30720,2]{0,1:T(2,128)} %param.31) | copy-start | bytes 737284
  3.3 13.5 %copy-start.1 = (f32[30720]{0:T(1024)S(1)}, f32[30720]{0:T(1024)}, u32[]{:S(2)}) copy-start(f32[30720]{0:T(1024)} %param.29) | copy-start | bytes 368644
  3.3 13.5 %copy-start.2 = (f32[30720]{0:T(1024)S(1)}, f32[30720]{0:T(1024)}, u32[]{:S(2)}) copy-start(f32[30720]{0:T(1024)} %param.30) | copy-start | bytes 368644
  3.3 13.5 %copy-start.3 = (s32[30720]{0:T(1024)S(1)}, s32[30720]{0:T(1024)}, u32[]{:S(2)}) copy-start(s32[30720]{0:T(1024)} %param.32) | copy-start | bytes 368644
  3.3 13.5 %copy-start.4 = (f32[5,900]{1,0:T(8,128)S(1)}, f32[5,900]{1,0:T(8,128)}, u32[]{:S(2)}) copy-start(f32[5,900]{1,0:T(8,128)} %coup_a.1) | copy-start | bytes 54004
  3.3 13.5 %copy-start.5 = (f32[5,900]{1,0:T(8,128)S(1)}, f32[5,900]{1,0:T(8,128)}, u32[]{:S(2)}) copy-start(f32[5,900]{1,0:T(8,128)} %coup_b.1) | copy-start | bytes 54004
  3.3 13.5 %copy-start.7 = (s32[2]{0:T(128)S(1)}, s32[2]{0:T(128)}, u32[]{:S(2)}) copy-start(s32[2]{0:T(128)} %blocks.1) | copy-start | bytes 28
  3.3 13.5 %copy-start.8 = (f32[1024]{0:T(1024)S(1)}, f32[1024]{0:T(1024)}, u32[]{:S(2)}) copy-start(f32[1024]{0:T(1024)} %param.33) | copy-start | bytes 12292
  3.3 13.5 %copy-start.9 = (f32[1024]{0:T(1024)S(1)}, f32[1024]{0:T(1024)}, u32[]{:S(2)}) copy-start(f32[1024]{0:T(1024)} %param.34) | copy-start | bytes 12292
  27.7 0.6 copy-start.6
  28.3 0.5 copy-start.10

commit v2 on v1

v2 whole, which is shorter than its diff:
```python
import functools
import math

import jax
import jax.numpy as jnp
from jax import lax
from jax.experimental import pallas as pl
from jax.experimental.pallas import tpu as pltpu
from jax.sharding import PartitionSpec as P

PAIRING = 1.0
TOP = 15
UPPER = 4
STEP = 256
MESH_ID = pl.DeviceIdType.MESH


def both(*conds):
    out = conds[0]
    for cond in conds[1:]:
        out = jnp.logical_and(out, cond)
    return out


def spread_kernel(block, dens, out, buf, rows_in, pieces, recv_sem, send_sem, local_sem):
    row = lax.axis_index("row")
    col = lax.axis_index("col")
    other = row + 1 - 2 * lax.rem(row, 2)
    level = col // 4
    half = lax.rem(col // 2, 2)
    core = lax.rem(col, 2)
    count, row_len, step = buf.shape[1:]
    features = dens.shape[1]

    src_level, src_half, src_core = block // 4, (block // 2) % 2, block % 2
    here = (src_level, src_half, src_core)

    top_src = col == TOP
    top_recv = level >= UPPER
    from_src = jnp.logical_and(level == UPPER, core == 1)
    top_from_row = jnp.where(jnp.logical_and(from_src, half == 0), other, row)
    top_from_col = jnp.where(core == 0, col + 1, jnp.where(from_src, TOP, col - 4))
    top_up = both(core == 1, level >= UPPER, level < 7)
    top_mate = both(core == 1, level >= UPPER)

    same = block == TOP
    src = col == block
    root_col = src_level * 4 + (1 - src_half) * 2
    root = col == root_col
    up_dst = both(level > src_level, level < UPPER)
    relay_zero = jnp.logical_and(src_level == 3, both(level == 0, core == 0))
    root_needs = jnp.logical_and(col > block, level == src_level)
    recv = jnp.logical_or(jnp.logical_or(col > block, root), relay_zero)
    if same:
        recv = col < 0
        src = col < 0
        root = col < 0
    src_dev = jnp.where(half == src_half, block, root_col)
    turn = 6 if src_level == 3 else UPPER
    on_mate = jnp.logical_and(core == 1, col > block)
    if src_level == 3:
        entry_up = both(level == UPPER, core == 0)
        entry_down = both(level == 0, core == 0)
        from_zero = both(level == 7, core == 0)
    else:
        entry_up = both(level == src_level + 1, core == 0)
        entry_down = both(level == 7, core == 0)
        from_zero = col < 0
    from_col = jnp.where(
        root,
        block,
        jnp.where(
            on_mate,
            col - 1,
            jnp.where(
                jnp.logical_or(entry_up, entry_down),
                src_dev,
                jnp.where(from_zero, half * 2, jnp.where(level >= turn, col + 4, col - 4)),
            ),
        ),
    )
    from_row = jnp.where(root, other, row)
    start = jnp.logical_or(src, root)
    down_entry_col = (0 if src_level == 3 else 28) + half * 2
    none = col < 0
    if same:
        sends = []
        root_send = none
    else:
        up_relay = both(core == 0, level > src_level, level < turn - 1)
        up = jnp.logical_or(start, up_relay)
        up_col = jnp.where(start, (src_level + 1) * 4 + half * 2, col + 4)
        down_relay = both(core == 0, level > turn)
        zero_relay = both(core == 0, level == 0) if src_level == 3 else none
        down = jnp.logical_or(jnp.logical_or(start, down_relay), zero_relay)
        down_col = jnp.where(start, down_entry_col, jnp.where(zero_relay, 28 + half * 2, col - 4))
        mate = jnp.logical_and(core == 0, col >= block)
        sends = [(up, up_col), (down, down_col), (mate, col + 1)]
        root_send = src

    barrier = pltpu.get_barrier_semaphore()

    @pl.when(top_recv)
    def _():
        pl.semaphore_signal(barrier, 1, device_id=(top_from_row, top_from_col), device_id_type=MESH_ID)

    @pl.when(recv)
    def _():
        pl.semaphore_signal(barrier, 1, device_id=(from_row, from_col), device_id_type=MESH_ID)

    one = lambda cond: jnp.where(cond, 1, 0)
    total = 2 * one(top_src) + one(top_up) + one(top_mate) + one(root_send)
    for cond, _ in sends:
        total = total + one(cond)

    def copy(which, slot, j, src_ref, to_row, to_col):
        return pltpu.make_async_remote_copy(
            src_ref=src_ref,
            dst_ref=buf.at[which, j],
            send_sem=send_sem.at[which, slot, j],
            recv_sem=recv_sem.at[which, j],
            device_id=(to_row, to_col),
            device_id_type=MESH_ID,
        )

    def held(which, j):
        return buf.at[which, j]

    def each(body):
        def step_of(j, carry):
            body(j)
            return carry

        lax.fori_loop(0, count, step_of, 0)

    any_src = jnp.logical_or(top_src, src)

    def load(k, r):
        rows = dens.at[pl.ds(pl.multiple_of(r * row_len, 8), row_len)]
        return pltpu.make_async_copy(rows, rows_in.at[k], local_sem.at[k])

    @pl.when(any_src)
    def _():
        load(0, row).start()
        load(1, other).start()
        load(0, row).wait()
        load(1, other).wait()
        for k in range(2):
            for j in range(count):
                width = min(step, features - j * step)
                pieces[k, j, :, 0:width] = rows_in[k, :, j * step : j * step + width]

    @pl.when(total > 0)
    def _():
        pl.semaphore_wait(barrier, total)

    @pl.when(top_src)
    def _():
        def send(j):
            copy(0, 0, j, pieces.at[0, j], row, UPPER * 4 + 3).start()
            copy(0, 1, j, pieces.at[1, j], other, UPPER * 4 + 1).start()

        each(send)

    if not same:

        @pl.when(src)
        def _():
            def send(j):
                copy(1, 3, j, pieces.at[1, j], other, root_col).start()
                for slot, (cond, to_col) in enumerate(sends):

                    @pl.when(cond)
                    def _():
                        copy(1, slot, j, pieces.at[0, j], row, to_col).start()

            each(send)

    if not same:

        @pl.when(jnp.logical_and(recv, core == 0))
        def _():
            def pass_on(j):
                copy(1, 0, j, held(1, j), row, col).wait_recv()
                for slot, (cond, to_col) in enumerate(sends):

                    @pl.when(cond)
                    def _():
                        copy(1, slot, j, held(1, j), row, to_col).start()

            each(pass_on)

    @pl.when(top_mate)
    def _():
        def pass_on(j):
            copy(0, 0, j, held(0, j), row, col).wait_recv()

            @pl.when(top_up)
            def _():
                copy(0, 1, j, held(0, j), row, col + 4).start()

            copy(0, 0, j, held(0, j), row, col - 1).start()

        each(pass_on)

    @pl.when(both(top_recv, core == 0))
    def _():
        each(lambda j: copy(0, 0, j, held(0, j), row, col).wait_recv())

    if not same:

        @pl.when(jnp.logical_and(recv, core == 1))
        def _():
            each(lambda j: copy(1, 0, j, held(1, j), row, col).wait_recv())

    def write(which, ref):
        return pltpu.make_async_copy(ref, out.at[which], local_sem.at[2 + which])

    for which, mine in ((0, top_src), (1, src)):

        @pl.when(mine)
        def _():
            write(which, pieces.at[0]).start()

        @pl.when(jnp.logical_not(mine))
        def _():
            write(which, buf.at[which]).start()

    @pl.when(top_src)
    def _():
        def wait(j):
            copy(0, 0, j, held(0, j), row, col).wait_send()
            copy(0, 1, j, held(0, j), row, col).wait_send()

        each(wait)

    @pl.when(top_mate)
    def _():
        each(lambda j: copy(0, 0, j, held(0, j), row, col).wait_send())

    @pl.when(top_up)
    def _():
        each(lambda j: copy(0, 1, j, held(0, j), row, col).wait_send())

    for slot, (cond, _) in enumerate(sends):

        @pl.when(cond)
        def _():
            each(lambda j: copy(1, slot, j, held(1, j), row, col).wait_send())

    if not same:

        @pl.when(src)
        def _():
            each(lambda j: copy(1, 3, j, held(1, j), row, col).wait_send())

    for which in range(2):
        write(which, buf.at[which]).wait()


def spread(block, row_len, dens):
    features = dens.shape[1]
    count = -(-features // STEP)
    return pl.pallas_call(
        functools.partial(spread_kernel, block),
        name=f"spread_{block}",
        out_shape=jax.ShapeDtypeStruct((2, count, row_len, STEP), dens.dtype),
        in_specs=[pl.BlockSpec(memory_space=pl.ANY)],
        out_specs=pl.BlockSpec(memory_space=pl.ANY),
        scratch_shapes=[
            pltpu.VMEM((2, count, row_len, STEP), dens.dtype),
            pltpu.VMEM((2, row_len, features), dens.dtype),
            pltpu.VMEM((2, count, row_len, STEP), dens.dtype),
            pltpu.SemaphoreType.DMA((2, count)),
            pltpu.SemaphoreType.DMA((2, 4, count)),
            pltpu.SemaphoreType.DMA((4,)),
        ],
        compiler_params=pltpu.CompilerParams(
            collective_id=block, has_side_effects=True, vmem_limit_bytes=8 * 1024 * 1024
        ),
    )(dens)


def split3(x):
    hi = x.astype(jnp.bfloat16)
    rest = x - hi.astype(jnp.float32)
    mid = rest.astype(jnp.bfloat16)
    low = (rest - mid.astype(jnp.float32)).astype(jnp.bfloat16)
    return hi, mid, low


def dot_t(a, b):
    return lax.dot_general(a, b, (((1,), (1,)), ((), ())), preferred_element_type=jnp.float32)


def pick(table, index):
    states = table.shape[1]
    hit = lax.broadcasted_iota(jnp.int32, (states, index.shape[1]), 0) == index
    hit = jnp.where(hit, 1.0, 0.0).astype(jnp.bfloat16)
    parts = jnp.dot(table, hit, preferred_element_type=jnp.float32)
    u = parts[0:1] + parts[1:2] + parts[2:3]
    v = parts[3:4] + parts[4:5] + parts[5:6]
    return u, v


def prepare_kernel(blocks, _, strength, energies, qp, label, amp_u, amp_v, col_out, row_out, win_f, win_i, near_f, near_i, sem):
    row = lax.axis_index("row")
    col = lax.axis_index("col")
    block_len = col_out.shape[1]
    row_len = row_out.shape[1]
    f32 = jnp.float32
    odd = lax.rem(col, 2)
    base = pl.multiple_of(col * block_len - 64 * odd, 128)
    moving = blocks[0] + blocks[1] - TOP
    firsts = [TOP * block_len + row * row_len, moving * block_len + row * row_len]
    nears = [pl.multiple_of(first // 128 * 128, 128) for first in firsts]
    copies = []
    wide = pl.ds(base, block_len + 64)
    for i, (src, dst) in enumerate(
        [
            (strength.at[:, wide], win_f),
            (qp.at[:, wide], win_i.at[pl.ds(0, 2)]),
            (label.at[:, wide], win_i.at[pl.ds(2, 1)]),
        ]
        + [
            pair
            for k in range(2)
            for pair in (
                (strength.at[:, pl.ds(nears[k], 256)], near_f.at[k, pl.ds(0, 1)]),
                (energies.at[:, pl.ds(nears[k], 256)], near_f.at[k, pl.ds(1, 1)]),
                (qp.at[:, pl.ds(nears[k], 256)], near_i.at[k, pl.ds(0, 2)]),
                (label.at[:, pl.ds(nears[k], 256)], near_i.at[k, pl.ds(2, 1)]),
            )
        ]
    ):
        copies.append(pltpu.make_async_copy(src, dst, sem.at[i]))
        copies[-1].start()
    table = jnp.concatenate(
        [t.astype(f32) for t in (*split3(amp_u[...]), *split3(amp_v[...]))] + [jnp.zeros((2, amp_u.shape[1]), f32)], 0
    ).astype(jnp.bfloat16)

    def factors(pairs):
        u_i, v_i = pick(table, pairs[0:1])
        u_j, v_j = pick(table, pairs[1:2])
        return u_i * v_j + v_i * u_j, u_i * u_j - v_i * v_j

    for copy in copies:
        copy.wait()

    def own(x):
        return jnp.where(odd == 1, x[:, 64:], x[:, :block_len])

    whole = own(win_i[...])
    anomal, direct = factors(whole[0:2])
    col_out[0:1, :] = anomal
    col_out[1:2, :] = direct
    col_out[2:3, :] = whole[2:3].astype(f32)
    col_out[3:4, :] = own(win_f[...])
    for k in range(2):
        block = (TOP, moving)[k]
        shift = firsts[k] - nears[k]
        ints = pltpu.roll(near_i[k], 256 - shift, axis=1)[:, :128]
        floats = pltpu.roll(near_f[k], 256 - shift, axis=1)[:, :128]
        anomal, direct = factors(ints[0:2])
        lane = lax.broadcasted_iota(jnp.int32, (1, 128), 1)
        diagonal = firsts[k] + lane - col * block_len
        packed = jnp.concatenate(
            [
                anomal,
                direct,
                ints[2:3].astype(f32),
                floats[1:2],
                floats[0:1],
                diagonal.astype(f32),
                jnp.full((1, 128), jnp.where(col >= block, 1.0, 0.0), f32),
                jnp.full((1, 128), jnp.where(blocks[k] == TOP, 1.0, 0.0), f32),
            ],
            0,
        )
        row_out[k] = jnp.concatenate([packed, jnp.zeros((120, 128), f32)], 0).T[:row_len]


def prepare(block_len, row_len, blocks, panels, strength, energies, qp, label, amp_u, amp_v):
    anywhere = pl.BlockSpec(memory_space=pl.ANY)
    vmem = pl.BlockSpec(memory_space=pltpu.VMEM)
    out = jax.ShapeDtypeStruct
    return pl.pallas_call(
        prepare_kernel,
        name="prepare",
        out_shape=(out((8, block_len), jnp.float32), out((2, row_len, 128), jnp.float32)),
        in_specs=[pl.BlockSpec(memory_space=pltpu.SMEM)] + [anywhere] * 5 + [vmem] * 2,
        out_specs=(vmem, vmem),
        scratch_shapes=[
            pltpu.VMEM((1, block_len + 64), jnp.float32),
            pltpu.VMEM((4, block_len + 64), jnp.int32),
            pltpu.VMEM((2, 8, 256), jnp.float32),
            pltpu.VMEM((2, 8, 256), jnp.int32),
            pltpu.SemaphoreType.DMA((11,)),
        ],
        compiler_params=pltpu.CompilerParams(vmem_limit_bytes=16 * 1024 * 1024),
    )(blocks, panels, strength, energies, qp, label, amp_u, amp_v)


def finish_kernel(
    panels,
    dens,
    coup_a,
    coup_b,
    col_in,
    row_in,
    mat_a,
    mat_b,
    response,
    mirror,
    weight,
    acc,
    resp_all,
    mir_pair,
    mir_all,
    resp_send,
    resp_recv,
    pair_send,
    pair_recv,
    mir_send,
    mir_recv,
):
    row = lax.axis_index("row")
    col = lax.axis_index("col")
    rows = lax.axis_size("row")
    cols = lax.axis_size("col")
    other = row + 1 - 2 * lax.rem(row, 2)
    deep = rows // 2
    z = row // 2
    row_len = mat_a.shape[1]
    block_len = dens.shape[0]
    features = dens.shape[1]
    total = block_len * cols

    barrier = pltpu.get_barrier_semaphore()

    def greet_col(d, _):
        pl.semaphore_signal(barrier, 1, device_id=(row, lax.rem(col + d, cols)), device_id_type=MESH_ID)
        return 0

    def greet_deep(d, _):
        to = lax.rem(z + d, deep) * 2 + lax.rem(row, 2)
        pl.semaphore_signal(barrier, 1, device_id=(to, col), device_id_type=MESH_ID)
        return 0

    lax.fori_loop(1, cols, greet_col, 0)
    lax.fori_loop(1, deep, greet_deep, 0)
    pl.semaphore_signal(barrier, 1, device_id=(other, col), device_id_type=MESH_ID)

    types, points = coup_a.shape
    for t in range(types):
        weight[0:1, t * points : (t + 1) * points] = coup_a[t : t + 1, :]
        weight[1:2, t * points : (t + 1) * points] = coup_b[t : t + 1, :]

    acc[...] = jnp.zeros_like(acc)

    def product(j, lo, size):
        at = pl.ds(lo, size)
        wa = weight[0:1, at]
        wb = weight[1:2, at]
        stack = []
        for k in range(2):
            p = jnp.concatenate([panels[k, j], panels[k, j + 1]], 1)[:, :size].astype(jnp.float32)
            stack += [p * wa, p * wb]
        weighted = jnp.concatenate(stack, 0).astype(jnp.bfloat16)
        acc[...] += dot_t(weighted, dens[:, at])

    def body(i, carry):
        product(2 * i, pl.multiple_of(i * 2 * STEP, 2 * STEP), 2 * STEP)
        return carry

    full = features // (2 * STEP)
    lax.fori_loop(0, full, body, 0)
    product(2 * full, full * 2 * STEP, features - full * 2 * STEP)

    col_anomal = col_in[0:1, :]
    col_direct = col_in[1:2, :]
    col_label = col_in[2:3, :]
    col_strength = col_in[3:4, :]
    lane = lax.broadcasted_iota(jnp.int32, (1, block_len), 1).astype(jnp.float32)
    mats = []
    for k in range(2):
        anomal, direct, lab, energy, stren, diagonal, active, _ = (row_in[k, :, i : i + 1] for i in range(8))
        agree = lab == col_label
        prod_a = acc[2 * k * row_len : (2 * k + 1) * row_len]
        prod_b = acc[(2 * k + 1) * row_len : (2 * k + 2) * row_len]
        a = prod_a + jnp.where(diagonal == lane, energy, 0.0)
        a = a + PAIRING * jnp.where(agree, anomal * col_anomal, 0.0)
        b = prod_b + PAIRING * jnp.where(agree, direct * col_direct, 0.0)
        a = jnp.where(active > 0.0, a, 0.0)
        b = jnp.where(active > 0.0, b, 0.0)
        both_ab = a + b
        down = jnp.sum(both_ab * stren, axis=0, keepdims=True)
        across = jnp.sum(both_ab * col_strength, axis=1, keepdims=True)
        mats.append((a, b, down, across))
    resp = []
    for k in range(2):
        is_top = row_in[k, :, 7:8] > 0.0
        mat_a[k] = jnp.where(is_top, mats[0][0], mats[1][0])
        mat_b[k] = jnp.where(is_top, mats[0][1], mats[1][1])
        mir_pair[0, k : k + 1, :] = jnp.where(is_top[0:1], mats[0][2], mats[1][2])
        resp.append(jnp.where(is_top, mats[0][3], mats[1][3]))
    wide_resp = jnp.concatenate(resp + [jnp.zeros((128 - 2 * row_len, 1), jnp.float32)], 0)
    resp_all[col] = jnp.broadcast_to(wide_resp, (128, 128)).T[0:1]

    pl.semaphore_wait(barrier, cols - 1 + deep - 1 + 1)

    def send_resp(d, _):
        pltpu.make_async_remote_copy(
            src_ref=resp_all.at[col],
            dst_ref=resp_all.at[col],
            send_sem=resp_send,
            recv_sem=resp_recv,
            device_id=(row, lax.rem(col + d, cols)),
            device_id_type=MESH_ID,
        ).start()
        return 0

    pair = pltpu.make_async_remote_copy(
        src_ref=mir_pair.at[0],
        dst_ref=mir_pair.at[1],
        send_sem=pair_send,
        recv_sem=pair_recv,
        device_id=(other, col),
        device_id_type=MESH_ID,
    )
    pair.start()
    lax.fori_loop(1, cols, send_resp, 0)
    pair.wait_recv()
    mir_all[z] = (mir_pair[0] + mir_pair[1]).astype(mir_all.dtype)

    def send_mir(d, _):
        to = lax.rem(z + d, deep) * 2 + lax.rem(row, 2)
        pltpu.make_async_remote_copy(
            src_ref=mir_all.at[z],
            dst_ref=mir_all.at[z],
            send_sem=mir_send,
            recv_sem=mir_recv,
            device_id=(to, col),
            device_id_type=MESH_ID,
        ).start()
        return 0

    lax.fori_loop(1, deep, send_mir, 0)

    def wait_all(ref, count, sem):
        some = ref.at[pl.ds(0, count)]
        pltpu.make_async_copy(some, some, sem).wait()

    wait_all(resp_all, cols - 1, resp_recv)
    r = jnp.sum(resp_all[...], axis=0) * (1.0 / math.sqrt(total))
    response[0:1, :] = r[:, :row_len]
    response[1:2, :] = r[:, row_len : 2 * row_len]
    wait_all(mir_all, deep - 1, mir_recv)
    m = jnp.sum(mir_all[...].astype(jnp.float32), axis=0) * (1.0 / math.sqrt(block_len))
    mirror[...] = m
    wait_all(resp_all, cols - 1, resp_send)
    wait_all(mir_all, deep - 1, mir_send)
    pair.wait_send()


def finish(rows, cols, panels, dens, coup_a, coup_b, col_in, row_in):
    row_len = panels.shape[2]
    block_len, features = dens.shape
    vmem = pl.BlockSpec(memory_space=pltpu.VMEM)
    out = jax.ShapeDtypeStruct
    f32 = jnp.float32
    return pl.pallas_call(
        finish_kernel,
        name="finish",
        out_shape=(
            out((2, row_len, block_len), f32),
            out((2, row_len, block_len), f32),
            out((2, row_len), f32),
            out((2, block_len), f32),
        ),
        in_specs=[vmem] * 6,
        out_specs=(vmem,) * 4,
        scratch_shapes=[
            pltpu.VMEM((8, features), f32),
            pltpu.VMEM((4 * row_len, block_len), f32),
            pltpu.VMEM((cols, 1, 128), f32),
            pltpu.VMEM((2, 2, block_len), f32),
            pltpu.VMEM((rows // 2, 2, block_len), jnp.bfloat16),
        ]
        + [pltpu.SemaphoreType.DMA] * 6,
        compiler_params=pltpu.CompilerParams(
            collective_id=TOP + 1, has_side_effects=True, vmem_limit_bytes=24 * 1024 * 1024
        ),
    )(panels, dens, coup_a, coup_b, col_in, row_in)


def on_device(
    densities, coupling_a, coupling_b, energies, strength, qp_index, kpi_label, amplitude_u, amplitude_v, panel_blocks
):
    rows = lax.axis_size("row")
    cols = lax.axis_size("col")
    block_len = densities.shape[0]
    row_len = block_len // rows
    flat = lambda x: x.reshape(1, -1)
    moving = panel_blocks[0] + panel_blocks[1] - TOP
    branches = [functools.partial(spread, block, row_len) for block in range(TOP + 1)]
    panels = lax.switch(moving, branches, densities)
    col_in, row_in = prepare(
        block_len,
        row_len,
        panel_blocks,
        panels,
        flat(strength),
        flat(energies),
        qp_index.T,
        flat(kpi_label),
        flat(amplitude_u),
        flat(amplitude_v),
    )
    return finish(rows, cols, panels, densities, coupling_a, coupling_b, col_in, row_in)


def solution(mesh):
    placed = (P("col", None), P(), P(), P(), P(), P(), P(), P(), P(), P())
    return jax.shard_map(
        on_device,
        mesh=mesh,
        in_specs=placed,
        out_specs=(P(None, "row", "col"), P(None, "row", "col"), P(None, "row"), P(None, "col")),
        check_vma=False,
    )
```

time: 72.3 us -> 63 us (0.87)
  Pallas kernels: 65.9 us -> 56.9 us
  local copies, waits for them, and re-layouts: 5 us -> 3.98 us
    pallas_call x1, Pallas kernels: 13.1 us -> 3.02 us  [spread(): pl.pallas_call(functools.partial(spread_kernel, block), name=f'spread_{bl...]
    pallas_call x2, Pallas kernels: 52.8 us -> 53.9 us  [the longest x1 51.5 us: finish(): pl.pallas_call(finish_kernel, name='finish', out_shape=(out((2, row_len,...]
    unnamed x24 -> x22, local copies, waits for them, and re-layouts: 3.69 us -> 2.67 us
where the time goes in v2:
time: 63 us; the launch traced here: 63.2 us
  Pallas kernels  56.9 us (90%)
  local copies, waits for them, and re-layouts  3.98 us (6%)
  between operations  2.1 us (3%)
    pallas_call x1, Pallas kernels, finish(): pl.pallas_call(finish_kernel, name='finish', out_shape=(out((2, row_len,...  51.5 us
    pallas_call x1, Pallas kernels, spread(): pl.pallas_call(functools.partial(spread_kernel, block), name=f'spread_{bl...  3.02 us
    unnamed x22, local copies, waits for them, and re-layouts  2.67 us
    pallas_call x1, Pallas kernels, prepare(): pl.pallas_call(prepare_kernel, name='prepare', out_shape=(out((8, block_l...  2.36 us
    slice x1, local copies, waits for them, and re-layouts, on_device(): moving = panel_blocks[0] + panel_blocks[1] - TOP  1.31 us

profile of v2, /device:TPU:6, one launch (start us, length us, event | category | flops | bytes accessed | tf_op | source)
XLA Modules:
  0.0 63.2 jit_solution(17514471439707024178)
XLA Ops:
  0.6 1.3 %fusion = (s32[1]{0:T(128)}, s32[1]{0:T(128)}) fusion(s32[2]{0:T(128)} %blocks.1), kind=kLoop, calls=%fused_computation | loop fusion | bytes 16 | tf_op jit(solution)/shard_map/slice | solution.py:605
  3.2 0.0 copy-start
  3.3 0.0 copy-start.1
  3.3 0.0 copy-start.2
  3.3 0.0 copy-start.3
  3.3 0.0 copy-start.6
  3.3 0.0 copy-start.7
  3.3 0.0 copy-start.8
  3.3 0.0 copy-start.4
  3.3 0.0 copy-start.5
  3.4 3.3 %conditional.1 = (bf16[2,18,40,256]{3,2,1,0:T(8,128)(2,1)S(1)}) conditional(s32[]{:T(128)} %bitcast, bf16[960,4500]{1,0:T(8,128)(2,1)} %dens.17, bf16[960,4500]{1,0:T(8,128)(2,1)} %dens.17, bf16[960,4500]{1,0:T(8,128)(2,1)} %dens.17, bf16[960,4500]{1,0:T(8,128)(2,1)} %dens.17, bf16[960,4500]{1,0:T(8,128)(2,1)} %dens.17, ...), branch_computations={%region_0.0_spmd, %region_1.0_spmd, %region_2.0_spmd, %region_3.0_... | conditional | bytes 8 | solution.py:607
  3.4 3.0 %spread_10.1 = bf16[2,18,40,256]{3,2,1,0:T(8,128)(2,1)S(1)} custom-call(bf16[960,4500]{1,0:T(8,128)(2,1)} %dens.11), custom_call_target="tpu_custom_call" | custom-call | tf_op jit(solution)/shard_map/cond/branch_10_fun/spread_10/pallas_call | solution.py:264
  6.6 0.0 copy-done
  6.6 0.0 copy-done.1
  6.6 0.0 copy-done.2
  6.7 0.0 copy-done.3
  6.7 0.0 copy-done.6
  6.7 0.0 copy-done.7
  6.7 0.0 copy-done.8
  6.7 2.4 %prepare.1 = (f32[8,960]{1,0:T(8,128)S(1)}, f32[2,40,128]{2,1,0:T(8,128)S(1)}) custom-call(s32[2]{0:T(128)S(1)} %copy-done.6, bf16[2,18,40,256]{3,2,1,0:T(8,128)(2,1)S(1)} %get-tuple-element.51._.panels, f32[1,30720]{1,0:T(1,128)S(1)} %bitcast.8, f32[1,30720]{1,0:T(1,128)S(1)} %bitcast.9, s32[2,30720]{1,0:T(2,128)S(1)} %bitcast.7, s32[1,30720]{1,0:T(1,128)S(1)} %bitcast.10, ...), custom_call_target="tpu_custom_call" | custom-call | tf_op jit(solution)/shard_map/prepare/pallas_call | solution.py:387
  9.1 0.0 copy-done.4
  9.1 0.0 copy-done.5
  9.1 51.5 %finish.1 = (f32[2,40,960]{2,1,0:T(8,128)S(1)}, f32[2,40,960]{2,1,0:T(8,128)S(1)}, f32[2,40]{1,0:T(2,128)S(1)}, f32[2,960]{1,0:T(2,128)S(1)}) custom-call(bf16[2,18,40,256]{3,2,1,0:T(8,128)(2,1)S(1)} %get-tuple-element.51._.panels, bf16[960,4500]{1,0:T(8,128)(2,1)} %dens.17, f32[5,900]{1,0:T(8,128)S(1)} %copy-done.4, f32[5,900]{1,0:T(8,128)S(1)} %copy-done.5, ...), custom_call_target="tpu_custom_call" | custom-call | tf_op jit(solution)/shard_map/finish/pallas_call | solution.py:572
  60.6 0.7 %copy.34 = f32[2,40,960]{2,1,0:T(8,128)} copy(f32[2,40,960]{2,1,0:T(8,128)S(1)} %get-tuple-element.47) | data formatting | bytes 614400
  61.3 0.7 %copy.35 = f32[2,40,960]{2,1,0:T(8,128)} copy(f32[2,40,960]{2,1,0:T(8,128)S(1)} %get-tuple-element.48) | data formatting | bytes 614400
  62.0 0.6 copy.36
  62.6 0.6 copy.37
Async XLA Ops:
  3.2 3.4 %copy-start = (s32[30720,2]{0,1:T(2,128)S(1)}, s32[30720,2]{0,1:T(2,128)}, u32[]{:S(2)}) copy-start(s32[30720,2]{0,1:T(2,128)} %param.31) | copy-start | bytes 737284
  3.3 3.4 %copy-start.1 = (f32[30720]{0:T(1024)S(1)}, f32[30720]{0:T(1024)}, u32[]{:S(2)}) copy-start(f32[30720]{0:T(1024)} %param.30) | copy-start | bytes 368644
  3.3 3.4 %copy-start.2 = (f32[30720]{0:T(1024)S(1)}, f32[30720]{0:T(1024)}, u32[]{:S(2)}) copy-start(f32[30720]{0:T(1024)} %param.29) | copy-start | bytes 368644
  3.3 3.4 %copy-start.3 = (s32[30720]{0:T(1024)S(1)}, s32[30720]{0:T(1024)}, u32[]{:S(2)}) copy-start(s32[30720]{0:T(1024)} %param.32) | copy-start | bytes 368644
  3.3 3.4 %copy-start.6 = (s32[2]{0:T(128)S(1)}, s32[2]{0:T(128)}, u32[]{:S(2)}) copy-start(s32[2]{0:T(128)} %blocks.1) | copy-start | bytes 28
  3.3 3.4 %copy-start.7 = (f32[1024]{0:T(1024)S(1)}, f32[1024]{0:T(1024)}, u32[]{:S(2)}) copy-start(f32[1024]{0:T(1024)} %param.33) | copy-start | bytes 12292
  3.3 3.4 %copy-start.8 = (f32[1024]{0:T(1024)S(1)}, f32[1024]{0:T(1024)}, u32[]{:S(2)}) copy-start(f32[1024]{0:T(1024)} %param.34) | copy-start | bytes 12292
  3.3 5.7 %copy-start.4 = (f32[5,900]{1,0:T(8,128)S(1)}, f32[5,900]{1,0:T(8,128)}, u32[]{:S(2)}) copy-start(f32[5,900]{1,0:T(8,128)} %coup_a.1) | copy-start | bytes 54004
  3.3 5.7 %copy-start.5 = (f32[5,900]{1,0:T(8,128)S(1)}, f32[5,900]{1,0:T(8,128)}, u32[]{:S(2)}) copy-start(f32[5,900]{1,0:T(8,128)} %coup_b.1) | copy-start | bytes 54004
